TPU v7x, 32 devices: a whole 2x2x4 slice. The times are simulated.
32 devices in a mesh: cache: 2 (over y), tp: 8 (over z, core), cand: 2 (over x).
Axes of the slice: x: 2, y: 2, z: 4, core: 2. Of those that a mesh axis runs over, the one named last changes fastest.
Arguments:
- prompt_inputs: bfloat16 [1536, 8192], P(('cache', 'cand')), may hold values from -6 to 6
- cand_inputs: bfloat16 [4096, 8192], P(('cache', 'cand'), 'tp'), may hold values from -6 to 6
- norm_gain: float32 [8192], replicated, may hold values from 0.1 to 1.9
- w_query: bfloat16 [8192, 8192], P('cache', 'tp'), may hold values from -0.0625 to 0.0625
- w_key: bfloat16 [8192, 1024], P('cache', 'tp'), may hold values from -0.0625 to 0.0625
- w_value: bfloat16 [8192, 1024], P('cache', 'tp'), may hold values from -0.0625 to 0.0625
- q_bias: float32 [8192], P('tp'), may hold values from -180 to 180
- k_bias: float32 [1024], P('tp'), may hold values from -3 to 8
- v_bias: float32 [1024], P('tp'), may hold values from -4 to 4
- cand_lengths: int32 [16], replicated, may hold values from 32 to 256, as said below
- prefix_ends: int32 [16], replicated, may hold values from 384 to 1536, as said below
Outputs:
- attn_out: bfloat16 [4096, 8192], P(('cache', 'cand'), 'tp')
Inputs may be any that keep to these rules, and one draw needn't show every extreme that they name: `cand_lengths`: at least one candidate has 256 tokens. `prefix_ends`: at least one candidate follows the whole prompt.
All inputs are finite; a program needn't handle non-finite values.
Results may differ from a plain program's by a relative error of at most 0.0075.
The roundings to bfloat16 on the way count: a program that leaves them out, or rounds other values in their place, can miss the bound.
Values may be sent and summed in bfloat16 or wider, within the bound.
A program may use at most 192 MiB of HBM per device.

v0:
```python
import jax
import jax.numpy as jnp
from jax import lax
from jax.sharding import PartitionSpec as P

D = 8192
HEADS = 64
KV_HEADS = 8
HEAD = 128
CANDS = 16
CLEN = 256
ROPE_THETA = 1000000.0
EPSILON = 1e-06


def rotate(tensor, positions):
    half_size = tensor.shape[-1] // 2
    inverse_freq = jnp.power(
        ROPE_THETA, -jnp.arange(half_size, dtype=jnp.float32) * 2.0 / tensor.shape[-1]
    )
    angles = positions.astype(jnp.float32)[:, None] * inverse_freq[None, :]
    cosine = jnp.cos(angles)[:, None, :]
    sine_part = jnp.sin(angles)[:, None, :]
    first_half = tensor[..., :half_size]
    second = tensor[..., half_size:]
    return jnp.concatenate(
        [first_half * cosine - second * sine_part, second * cosine + first_half * sine_part],
        axis=-1,
    )


def row_lookup(row_ids, table):
    chosen = (row_ids // CLEN)[:, None] == jnp.arange(CANDS, dtype=jnp.int32)[None, :]
    return jnp.sum(jnp.where(chosen, table[None, :], 0), axis=1)


def key_visible(row_ids, key_index, prefix_row, prompt_dev, cand_dev):
    unit_rows = prompt_dev + cand_dev
    key_owner = key_index // unit_rows
    key_offset = key_index % unit_rows
    is_prompt = key_offset < prompt_dev
    prompt_pos = key_owner * prompt_dev + key_offset
    cand_row = key_owner * cand_dev + key_offset - prompt_dev
    seen_prompt = prompt_pos[None, :] < prefix_row[:, None]
    seen_cand = ((cand_row // CLEN)[None, :] == (row_ids // CLEN)[:, None]) & (
        cand_row[None, :] <= row_ids[:, None]
    )
    return jnp.where(is_prompt[None, :], seen_prompt, seen_cand)


def attend_block(queries, key_rows, value_rows, visible, running):
    maxima, totals, accumulated = running
    scores = jnp.einsum(
        "rgqd,ngd->rgqn", queries, key_rows, preferred_element_type=jnp.float32
    ) * queries.shape[-1] ** (-0.5)
    visible_four = visible[:, None, None, :]
    new_maxima = jnp.maximum(maxima, jnp.max(jnp.where(visible_four, scores, -1e30), axis=-1))
    weights = jnp.exp(jnp.where(visible_four, scores - new_maxima[..., None], -jnp.inf))
    rescale = jnp.exp(maxima - new_maxima)
    totals = totals * rescale + jnp.sum(weights, axis=-1)
    accumulated = accumulated * rescale[..., None] + jnp.einsum(
        "rgqn,ngd->rgqd",
        weights.astype(jnp.bfloat16),
        value_rows,
        preferred_element_type=jnp.float32,
    )
    return (new_maxima, totals, accumulated)


def block_size(total_rows, unit_rows):
    for multiple in (4, 2, 1):
        if total_rows > multiple * unit_rows and total_rows % (multiple * unit_rows) == 0:
            return multiple * unit_rows
    return total_rows


def per_device(
    prompt_inputs,
    cand_inputs,
    norm_gain,
    w_query,
    w_key,
    w_value,
    q_bias,
    k_bias,
    v_bias,
    cand_lengths,
    prefix_ends,
):
    prompt_dev = prompt_inputs.shape[0]
    cand_dev = cand_inputs.shape[0]
    head_size = HEAD
    kv_local = w_key.shape[1] // head_size
    groups = HEADS // KV_HEADS
    kv_width = kv_local * head_size
    joined = lax.axis_index("cache") * lax.axis_size("cand") + lax.axis_index("cand")
    widened_p = prompt_inputs.astype(jnp.float32)
    normed_p = (
        widened_p
        * lax.rsqrt(jnp.mean(widened_p * widened_p, axis=-1, keepdims=True) + EPSILON)
        * norm_gain
    ).astype(jnp.bfloat16)
    widened_c = cand_inputs.astype(jnp.float32)
    squares = lax.psum(jnp.sum(widened_c * widened_c, axis=-1), "tp")
    part_width = cand_inputs.shape[1]
    gain_part = lax.dynamic_slice_in_dim(norm_gain, lax.axis_index("tp") * part_width, part_width)
    normed_part = (widened_c * lax.rsqrt(squares / D + EPSILON)[:, None] * gain_part).astype(
        jnp.bfloat16
    )
    normed_c = lax.all_gather(normed_part, "tp", axis=1, tiled=True)
    row_ids = joined * cand_dev + jnp.arange(cand_dev, dtype=jnp.int32)
    prefix_row = row_lookup(row_ids, prefix_ends)
    length_row = row_lookup(row_ids, cand_lengths)
    cand_pos = prefix_row + row_ids % CLEN
    prompt_pos = joined * prompt_dev + jnp.arange(prompt_dev, dtype=jnp.int32)
    kv_start = (
        jnp.zeros((prompt_dev, 2 * kv_width), jnp.float32),
        jnp.zeros((cand_dev, 2 * kv_width), jnp.float32),
    )
    initial = (kv_start[0], kv_start[1], jnp.zeros((cand_dev, w_query.shape[1]), jnp.float32))
    piece_key = lax.all_gather(w_key, "cache", axis=0, tiled=True)
    piece_value = lax.all_gather(w_value, "cache", axis=0, tiled=True)
    piece_query = lax.all_gather(w_query, "cache", axis=0, tiled=True)
    key_value = jnp.concatenate([piece_key, piece_value], axis=1)
    kv_prompt = jnp.dot(normed_p, key_value, preferred_element_type=jnp.float32)
    kv_cand = jnp.dot(normed_c, key_value, preferred_element_type=jnp.float32)
    q_cand = jnp.dot(normed_c, piece_query, preferred_element_type=jnp.float32)
    keys_p = rotate(
        (kv_prompt[:, :kv_width] + k_bias).reshape(prompt_dev, kv_local, head_size), prompt_pos
    ).astype(jnp.bfloat16)
    values_p = (
        (kv_prompt[:, kv_width:] + v_bias)
        .astype(jnp.bfloat16)
        .reshape(prompt_dev, kv_local, head_size)
    )
    keys_c = rotate(
        (kv_cand[:, :kv_width] + k_bias).reshape(cand_dev, kv_local, head_size), cand_pos
    ).astype(jnp.bfloat16)
    values_c = (
        (kv_cand[:, kv_width:] + v_bias).astype(jnp.bfloat16).reshape(cand_dev, kv_local, head_size)
    )
    queries = rotate(
        (q_cand + q_bias).reshape(cand_dev, kv_local * groups, head_size), cand_pos
    ).astype(jnp.bfloat16)
    queries = queries.reshape(cand_dev, kv_local, groups, head_size)
    keys_all = jnp.concatenate([keys_p, keys_c], axis=0)
    values_all = jnp.concatenate([values_p, values_c], axis=0)
    unit_rows = prompt_dev + cand_dev
    initial = (
        jnp.full((cand_dev, kv_local, groups), -1e30, jnp.float32),
        jnp.zeros((cand_dev, kv_local, groups), jnp.float32),
        jnp.zeros((cand_dev, kv_local, groups, head_size), jnp.float32),
    )
    piece_key = lax.all_gather(keys_all, ("cache", "cand"), axis=0, tiled=True)
    piece_value = lax.all_gather(values_all, ("cache", "cand"), axis=0, tiled=True)
    piece_rows = piece_key.shape[0]
    block_rows = block_size(piece_rows, unit_rows)

    def advance(turn_index, inner):
        first_row = turn_index * block_rows
        key_block = lax.dynamic_slice_in_dim(piece_key, first_row, block_rows, 0)
        value_block = lax.dynamic_slice_in_dim(piece_value, first_row, block_rows, 0)
        key_index = first_row + jnp.arange(block_rows, dtype=jnp.int32)
        visible = key_visible(row_ids, key_index, prefix_row, prompt_dev, cand_dev)
        return attend_block(queries, key_block, value_block, visible, inner)

    maxima, totals, accumulated = lax.fori_loop(0, piece_rows // block_rows, advance, initial)
    result = accumulated / totals[..., None]
    valid_rows = row_ids % CLEN < length_row
    result = jnp.where(valid_rows[:, None, None, None], result, 0.0).astype(jnp.bfloat16)
    return result.reshape(cand_dev, kv_local * groups * head_size)


def solution(mesh):
    placed = (
        P(("cache", "cand"), None),
        P(("cache", "cand"), "tp"),
        P(),
        P("cache", "tp"),
        P("cache", "tp"),
        P("cache", "tp"),
        P("tp"),
        P("tp"),
        P("tp"),
        P(),
        P(),
    )
    return jax.shard_map(
        per_device,
        mesh=mesh,
        in_specs=placed,
        out_specs=P(("cache", "cand"), "tp"),
        check_vma=False,
    )
```

profile of v0, /device:TPU:0, one launch (start us, length us, event | category | flops | bytes accessed | tf_op | source)
XLA Modules:
  0.0 713.0 jit_solution(11202659701899215689)
XLA Ops:
  6.5 0.0 all-gather.7.cloned.1.call-start
  6.5 0.7 all-gather.7.cloned.1.call-update
  7.3 0.0 all-gather.9.cloned.1.call-start
  7.3 0.7 all-gather.9.cloned.1.call-update
  8.0 0.0 all-gather.11.cloned.1.call-start
  8.1 0.7 dynamic_slice.25
  8.8 2.1 fusion.46
  10.8 18.1 %psum.7 = f32[1024]{0:T(1024)S(1)} all-reduce(f32[1024]{0:T(1024)S(1)} %fusion.46), channel_id=1, replica_groups=mesh['cache'=2,'tp'=8,'cand'=2] {'tp'}, use_global_device_ids=true, to_apply=%region_3.4 | all-reduce | flops 1024 | bytes 8192 | tf_op jit(solution)/shard_map/psum | solution.py:104
  28.9 0.0 copy-done
  28.9 1.9 fusion.48
  30.8 0.0 all-gather.11.cloned.1.call-update
  30.8 0.0 copy-start.7
  30.9 0.0 copy-start.8
  30.9 0.0 all-gather.15.cloned.1.call-start
  30.9 0.5 all-gather.15.cloned.1.call-update
  31.4 0.0 all-gather.13.cloned.1.call-start
  31.5 0.0 copy-done.7
  31.6 0.0 copy-done.8
  31.6 0.7 select_reduce_fusion.1
  32.2 4.1 fusion.39
  36.3 0.7 add_convert_fusion.1
  37.0 7.7 %all-gather.7.cloned.1.call-done = bf16[8192,128]{1,0:T(8,128)(2,1)} async-done(((bf16[4096,128]{1,0:T(8,128)(2,1)}), bf16[8192,128]{1,0:T(8,128)(2,1)}) %all-gather.7.cloned.1.call-update) | async-done | bytes 2097168 | tf_op jit(solution)/shard_map/all_gather | solution.py:121
  44.7 3.1 constant_dynamic-update-slice_fusion.1
  47.9 31.5 %all-gather.9.cloned.1.call-done = bf16[8192,128]{1,0:T(8,128)(2,1)} async-done(((bf16[4096,128]{1,0:T(8,128)(2,1)}), bf16[8192,128]{1,0:T(8,128)(2,1)}) %all-gather.9.cloned.1.call-update) | async-done | bytes 2097168 | tf_op jit(solution)/shard_map/all_gather | solution.py:122
  79.4 3.1 constant_dynamic-update-slice_fusion
  82.5 6.6 fusion.42
  89.1 0.0 copy-done.4
  89.1 0.0 copy-done.5
  89.1 0.1 fusion.72
  89.2 0.4 fusion.69
  89.7 142.4 %all-gather.11.cloned.1.call-done = bf16[1024,8192]{1,0:T(8,128)(2,1)} async-done(((bf16[1024,1024]{1,0:T(8,128)(2,1)}), bf16[1024,8192]{1,0:T(8,128)(2,1)}) %all-gather.11.cloned.1.call-update) | async-done | bytes 16777232 | tf_op jit(solution)/shard_map/all_gather | solution.py:110
  232.1 10.6 %fusion.80 = f32[1024,256]{0,1:T(8,128)S(1)} fusion(bf16[1024,8192]{1,0:T(8,128)(2,1)} %all-gather.11.cloned.1.call-done, bf16[8192,256]{1,0:T(8,128)(2,1)} %constant_dynamic-update-slice_fusion), kind=kOutput, calls=%fused_computation.138 | convolution fusion | flops 4294967296 | bytes 22020096 | tf_op jit(solution)/shard_map/dot_general | solution.py:126
  242.7 0.0 copy-start.9
  242.7 0.1 fusion.61
  242.8 1.2 fusion.58
  244.0 0.8 maximum_maximum_fusion
  244.8 0.0 all-gather.13.cloned.1.call-update
  244.8 0.2 all-gather.17.cloned.1.call-start
  245.0 0.6 fusion.78
  245.6 1.9 multiply_cosine_fusion
  247.5 0.8 pad_maximum_fusion.1
  248.3 0.0 all-gather.17.cloned.1.call-update
  248.3 182.3 %all-gather.15.cloned.1.call-done = bf16[8192,1024]{1,0:T(8,128)(2,1)} async-done(((bf16[4096,1024]{1,0:T(8,128)(2,1)}), bf16[8192,1024]{1,0:T(8,128)(2,1)}) %all-gather.15.cloned.1.call-update) | async-done | bytes 16777232 | tf_op jit(solution)/shard_map/all_gather | solution.py:123
  430.6 23.4 %convolution_add_fusion = f32[1024,1024]{0,1:T(8,128)S(1)} fusion(bf16[1024,8192]{1,0:T(8,128)(2,1)} %all-gather.11.cloned.1.call-done, bf16[8192,1024]{1,0:T(8,128)(2,1)} %all-gather.15.cloned.1.call-done, f32[1024]{0:T(1024)S(1)} %copy-done.9), kind=kOutput, calls=%fused_computation.76 | convolution fusion | flops 17180917760 | bytes 37752832 | tf_op jit(solution)/shard_map/dot_general | solution.py:127
  454.0 1.7 fusion.79
  455.7 3.8 copy.30
  459.5 2.7 copy.31
  462.2 4.6 fusion.49
  466.9 2.5 pad_maximum_fusion
  469.3 24.2 %all-gather.17.cloned.1.call-done = bf16[5632,1,128]{0,2,1:T(8,128)(2,1)} async-done(((bf16[1408,1,128]{0,2,1:T(8,128)(2,1)}), bf16[5632,1,128]{0,2,1:T(8,128)(2,1)}) %all-gather.17.cloned.1.call-update) | async-done | bytes 1441808 | tf_op jit(solution)/shard_map/all_gather | solution.py:155
  493.5 207.2 %while.23 = (s32[]{:T(128)}, f32[1024,1,8]{0,2,1:T(8,128)S(1)}, f32[1024,1,8]{0,2,1:T(8,128)}, f32[1024,1,8,128]{0,3,2,1:T(8,128)}, s32[1024]{0:T(1024)}, /*inde...) while((s32[]{:T(128)}, f32[1024,1,8]{0,2,1:T(8,128)S(1)}, ...), condition=%wide.region_8.9_spmd.clone.clone.clone, body=%wide.region_5.8_spmd.clone.clone.clone.sunk | while | flops 12082698240 | bytes 301176576 | solution.py:167
  493.7 5.0 and_select_fusion.2
  498.7 33.8 %fusion.97 = (f32[1024,8]{0,1:T(8,128)S(1)}, f32[2816,1024,8]{1,0,2:T(8,128)}) fusion(pred[1024,2816]{0,1:T(8,128)(4,1)S(1)} %and_select_fusion.2, bf16[1024,1,8,128]{3,0,2,1:T(8,128)(2,1)} %get-tuple-element.550, bf16[5632,1,128]{0,2,1:T(8,128)(2,1)} %get-tuple-element.549, s32[]{:T(128)S(6)} %select_n.299), kind=kOutput, calls=%fused_computation.5.clone.1 | convolution fusion | flops 5974777856 | bytes 98009088 | tf_op jit(solution)/shard_map/while/body/eval_jaxpr/rgqd,ngd->rgqn/dot_general | solution.py:53
  532.5 34.8 %bitcast_add_fusion.5 = f32[1024,1,8,128]{0,3,2,1:T(8,128)} fusion(f32[1024,1,8,128]{0,3,2,1:T(8,128)} %get-tuple-element.534, f32[2816,1024,8]{1,0,2:T(8,128)} %get-tuple-element.516, f32[1024,8]{0,1:T(8,128)S(1)} %bitcast.98, pred[1024,2816]{0,1:T(8,128)(4,1)S(1)} %and_select_fusion.2, f32[1024,8]{0,1:T(8,128)S(1)} %get-tuple-element.517, ...), kind=kOutput, calls=%fused_computation.14.clone.1 | convolution fusion | flops 6001000448 | bytes 104333320 | tf_op jit(solution)/shard_map/while/body/eval_jaxpr/rgqn,ngd->rgqd/dot_general | solution.py:61
  567.3 28.8 %fusion.99 = f32[1024,8]{0,1:T(8,128)S(1)} fusion(f32[2816,1024,8]{1,0,2:T(8,128)} %get-tuple-element.516, f32[1024,8]{0,1:T(8,128)S(1)} %bitcast.99, pred[1024,2816]{0,1:T(8,128)(4,1)S(1)} %and_select_fusion.2), kind=kLoop, calls=%fused_computation.9.clone.1 | loop fusion | flops 92266496 | bytes 95223808 | tf_op jit(solution)/shard_map/while/body/eval_jaxpr/reduce_sum | solution.py:60
  596.2 0.0 copy-start.2
  596.2 0.6 copy-done.2
  597.0 5.0 and_select_fusion.2
  602.0 33.8 %fusion.97 = (f32[1024,8]{0,1:T(8,128)S(1)}, f32[2816,1024,8]{1,0,2:T(8,128)}) fusion(pred[1024,2816]{0,1:T(8,128)(4,1)S(1)} %and_select_fusion.2, bf16[1024,1,8,128]{3,0,2,1:T(8,128)(2,1)} %get-tuple-element.550, bf16[5632,1,128]{0,2,1:T(8,128)(2,1)} %get-tuple-element.549, s32[]{:T(128)S(6)} %select_n.299), kind=kOutput, calls=%fused_computation.5.clone.1 | convolution fusion | flops 5974777856 | bytes 98009088 | tf_op jit(solution)/shard_map/while/body/eval_jaxpr/rgqd,ngd->rgqn/dot_general | solution.py:53
  635.8 35.4 %bitcast_add_fusion.5 = f32[1024,1,8,128]{0,3,2,1:T(8,128)} fusion(f32[1024,1,8,128]{0,3,2,1:T(8,128)} %get-tuple-element.534, f32[2816,1024,8]{1,0,2:T(8,128)} %get-tuple-element.516, f32[1024,8]{0,1:T(8,128)S(1)} %bitcast.98, pred[1024,2816]{0,1:T(8,128)(4,1)S(1)} %and_select_fusion.2, f32[1024,8]{0,1:T(8,128)S(1)} %get-tuple-element.517, ...), kind=kOutput, calls=%fused_computation.14.clone.1 | convolution fusion | flops 6001000448 | bytes 104333320 | tf_op jit(solution)/shard_map/while/body/eval_jaxpr/rgqn,ngd->rgqd/dot_general | solution.py:61
  671.2 28.8 %fusion.99 = f32[1024,8]{0,1:T(8,128)S(1)} fusion(f32[2816,1024,8]{1,0,2:T(8,128)} %get-tuple-element.516, f32[1024,8]{0,1:T(8,128)S(1)} %bitcast.99, pred[1024,2816]{0,1:T(8,128)(4,1)S(1)} %and_select_fusion.2), kind=kLoop, calls=%fused_computation.9.clone.1 | loop fusion | flops 92266496 | bytes 95223808 | tf_op jit(solution)/shard_map/while/body/eval_jaxpr/reduce_sum | solution.py:60
  700.1 0.6 copy-done.2
  700.7 2.8 select_convert_fusion
  703.6 2.6 copy.28
  (40 shorter events, 0.4 us)
Async XLA Ops:
  6.5 22.4 %copy-start = (bf16[1024,1024]{1,0:T(8,128)(2,1)S(1)}, bf16[1024,1024]{1,0:T(8,128)(2,1)}, u32[]{:S(2)}) copy-start(bf16[1024,1024]{1,0:T(8,128)(2,1)} %param.14) | copy-start | bytes 6291460
  6.5 38.2 %all-gather.7.cloned.1.call-start = ((), (), s32[]{:S(2)}) async-start(), calls=%async_computation | async-start | bytes 3145728 | tf_op jit(solution)/shard_map/all_gather | solution.py:121
  7.3 72.1 %all-gather.9.cloned.1.call-start = ((), (), s32[]{:S(2)}) async-start(), calls=%async_computation.1 | async-start | bytes 3145728 | tf_op jit(solution)/shard_map/all_gather | solution.py:122
  8.0 224.1 %all-gather.11.cloned.1.call-start = ((), (), s32[]{:S(2)}) async-start(), calls=%async_computation.2 | async-start | bytes 18874368 | tf_op jit(solution)/shard_map/all_gather | solution.py:110
  30.8 0.7 copy-start.7
  30.9 0.7 copy-start.8
  30.9 399.7 %all-gather.15.cloned.1.call-start = ((), (), s32[]{:S(2)}) async-start(), calls=%async_computation.4 | async-start | bytes 25165824 | tf_op jit(solution)/shard_map/all_gather | solution.py:123
  31.4 437.9 %all-gather.13.cloned.1.call-start = ((), (), s32[]{:S(2)}) async-start(), calls=%async_computation.3 | async-start | bytes 1802240 | tf_op jit(solution)/shard_map/all_gather | solution.py:154
  37.0 45.4 %copy-start.6 = (f32[8192]{0:T(1024)S(1)}, f32[8192]{0:T(1024)}, u32[]{:S(2)}) copy-start(f32[8192]{0:T(1024)} %param.15) | copy-start | bytes 98308
  82.5 6.6 copy-start.4
  82.5 6.6 copy-start.5
  242.7 187.9 %copy-start.9 = (f32[1024]{0:T(1024)S(1)}, f32[1024]{0:T(1024)}, u32[]{:S(2)}) copy-start(f32[1024]{0:T(1024)} %param.19) | copy-start | bytes 12292
  244.8 248.8 %all-gather.17.cloned.1.call-start = ((), (), s32[]{:S(2)}) async-start(), calls=%async_computation.5 | async-start | bytes 1802240 | tf_op jit(solution)/shard_map/all_gather | solution.py:155
  493.5 207.2 %copy-start.3 = (pred[1024]{0:T(1024)(128)(4,1)S(1)}, pred[1024]{0:T(1024)(128)(4,1)}, u32[]{:S(2)}) copy-start(pred[1024]{0:T(1024)(128)(4,1)} %fusion.78) | copy-start | bytes 3076
  567.3 28.9 %copy-start.1 = (f32[1024,1,8]{0,2,1:T(8,128)S(1)}, f32[1024,1,8]{0,2,1:T(8,128)}, u32[]{:S(2)}) copy-start(f32[1024,1,8]{0,2,1:T(8,128)} %get-tuple-element.533) | copy-start | bytes 98308 | tf_op jit(solution)/shard_map/while
  596.2 0.6 copy-start.2
  671.2 28.9 %copy-start.1 = (f32[1024,1,8]{0,2,1:T(8,128)S(1)}, f32[1024,1,8]{0,2,1:T(8,128)}, u32[]{:S(2)}) copy-start(f32[1024,1,8]{0,2,1:T(8,128)} %get-tuple-element.533) | copy-start | bytes 98308 | tf_op jit(solution)/shard_map/while
  700.1 0.6 copy-start.2
Sparse Core Ops, SparseCore 0:
  8.9 35.8 all-gather.6
  46.3 33.0 all-gather.8
  81.0 151.0 all-gather.10
  233.5 197.0 all-gather.14
  432.3 29.7 all-gather.12
  463.7 29.7 all-gather.16
where the time goes:
time: 714 us; the launch traced here: 713 us
  waiting for transfers between devices  390 us (55%)
  matrix products  178 us (25%)
  other arithmetic  93.2 us (13%)
  local copies, waits for them, and re-layouts  18.9 us (3%)
  blocking collectives  18.1 us (3%)
  between operations  13.7 us (2%)
    all_gather x1, waiting for transfers between devices, per_device(): piece_query = lax.all_gather(w_query, 'cache', axis=0, tiled=True)  182 us
    all_gather x1, waiting for transfers between devices, per_device(): normed_c = lax.all_gather(normed_part, 'tp', axis=1, tiled=True)  142 us
    dot_general x2, matrix products, attend_block(): jnp.einsum('rgqn,ngd->rgqd', weights.astype(jnp.bfloat16), value_rows, pr...  70.2 us
    dot_general x2, matrix products, attend_block(): jnp.einsum('rgqd,ngd->rgqn', queries, key_rows, preferred_element_type=jn...  67.6 us
    reduce_sum x2, other arithmetic, attend_block(): totals = totals * rescale + jnp.sum(weights, axis=-1)  57.7 us
    all_gather x1, waiting for transfers between devices, per_device(): piece_value = lax.all_gather(w_value, 'cache', axis=0, tiled=True)  31.5 us
    all_gather x1, waiting for transfers between devices, per_device(): lax.all_gather(values_all, ('cache', 'cand'), axis=0, tiled=True)  24.2 us
    dot_general x1, matrix products, per_device(): q_cand = jnp.dot(normed_c, piece_query, preferred_element_type=jnp.float32)  23.4 us
  transfers between devices with their start and end apart: 6, of which 5 were waited for; matrix products, arithmetic and copies ran while one was open for 11% of the time, Pallas kernels for 0%

commit v1 on v0

--- a/solution.py
+++ b/solution.py
@@ -11,6 +11,16 @@
 CLEN = 256
 ROPE_THETA = 1000000.0
 EPSILON = 1e-06
+
+
+def pass_along(shard, axis, dim):
+    size = lax.axis_size(axis)
+    held, blocks = (shard, [shard])
+    for _ in range(size - 1):
+        held = lax.ppermute(held, axis, [(i, (i + 1) % size) for i in range(size)])
+        blocks.insert(0, held)
+    row_of_blocks = jnp.concatenate(blocks, axis=dim)
+    return jnp.roll(row_of_blocks, (lax.axis_index(axis) + 1) * shard.shape[dim], axis=dim)
 
 
 def rotate(tensor, positions):
@@ -107,7 +117,7 @@
     normed_part = (widened_c * lax.rsqrt(squares / D + EPSILON)[:, None] * gain_part).astype(
         jnp.bfloat16
     )
-    normed_c = lax.all_gather(normed_part, "tp", axis=1, tiled=True)
+    normed_c = pass_along(normed_part, "tp", 1)
     row_ids = joined * cand_dev + jnp.arange(cand_dev, dtype=jnp.int32)
     prefix_row = row_lookup(row_ids, prefix_ends)
     length_row = row_lookup(row_ids, cand_lengths)

time: 714 us -> 563 us (0.79)
  waiting for transfers between devices: 390 us -> 198 us
  local copies, waits for them, and re-layouts: 18.9 us -> 58.6 us
    all_gather x1, waiting for transfers between devices: 182 us -> 0.02 us  [per_device(): piece_query = lax.all_gather(w_query, 'cache', axis=0, tiled=True)]
    ppermute x0 -> x7, waiting for transfers between devices: none -> 175 us  [pass_along(): held = lax.ppermute(held, axis, [(i, (i + 1) % size) for i in range(size)])]
    all_gather x1 -> x0, waiting for transfers between devices: 142 us -> none  [per_device(): normed_c = lax.all_gather(normed_part, 'tp', axis=1, tiled=True)]
    unnamed x19 -> x43, local copies, waits for them, and re-layouts: 9.71 us -> 49.3 us
    all_gather x1, waiting for transfers between devices: 31.5 us -> 0.01 us  [per_device(): piece_value = lax.all_gather(w_value, 'cache', axis=0, tiled=True)]
    all_gather x1, waiting for transfers between devices: 24.2 us -> 0.01 us  [per_device(): lax.all_gather(values_all, ('cache', 'cand'), axis=0, tiled=True)]
    all_gather x1, waiting for transfers between devices: 0.01 us -> 22.3 us  [per_device(): piece_key = lax.all_gather(keys_all, ('cache', 'cand'), axis=0, tiled=True)]
    all_gather x1, waiting for transfers between devices: 7.69 us -> 0.01 us  [per_device(): piece_key = lax.all_gather(w_key, 'cache', axis=0, tiled=True)]
  transfers between devices with their start and end apart: 6 -> 12, of which waited for: 5 -> 8; matrix products, arithmetic and copies ran while one was open for 11% -> 21% of each run, Pallas kernels for 0% -> 0%
where the time goes in v1:
time: 563 us; the launch traced here: 562 us
  waiting for transfers between devices  198 us (35%)
  matrix products  176 us (31%)
  other arithmetic  96.9 us (17%)
  local copies, waits for them, and re-layouts  58.6 us (10%)
  blocking collectives  18.1 us (3%)
  between operations  13.4 us (2%)
    ppermute x7, waiting for transfers between devices, pass_along(): held = lax.ppermute(held, axis, [(i, (i + 1) % size) for i in range(size)])  175 us
    dot_general x2, matrix products, attend_block(): jnp.einsum('rgqn,ngd->rgqd', weights.astype(jnp.bfloat16), value_rows, pr...  70.1 us
    dot_general x2, matrix products, attend_block(): jnp.einsum('rgqd,ngd->rgqn', queries, key_rows, preferred_element_type=jn...  67.6 us
    reduce_sum x2, other arithmetic, attend_block(): totals = totals * rescale + jnp.sum(weights, axis=-1)  57.7 us
    unnamed x43, local copies, waits for them, and re-layouts  49.3 us
    dot_general x1, matrix products, per_device(): q_cand = jnp.dot(normed_c, piece_query, preferred_element_type=jnp.float32)  23.4 us
    all_gather x1, waiting for transfers between devices, per_device(): piece_key = lax.all_gather(keys_all, ('cache', 'cand'), axis=0, tiled=True)  22.3 us
    psum x1, blocking collectives, per_device(): squares = lax.psum(jnp.sum(widened_c * widened_c, axis=-1), 'tp')  18.1 us
  transfers between devices with their start and end apart: 12, of which 8 were waited for; matrix products, arithmetic and copies ran while one was open for 21% of the time, Pallas kernels for 0%

profile of v1, /device:TPU:0, one launch (start us, length us, event | category | flops | bytes accessed | tf_op | source)
XLA Modules:
  0.0 561.8 jit_solution(13245609389651759619)
XLA Ops:
  6.5 0.7 all-gather.6.cloned.1.call-update
  7.3 0.7 dynamic_slice.29
  8.0 2.1 fusion.50
  10.1 18.1 %psum.7 = f32[1024]{0:T(1024)S(1)} all-reduce(f32[1024]{0:T(1024)S(1)} %fusion.50), channel_id=1, replica_groups=mesh['cache'=2,'tp'=8,'cand'=2] {'tp'}, use_global_device_ids=true, to_apply=%region_3.4 | all-reduce | flops 1024 | bytes 8192 | tf_op jit(solution)/shard_map/psum | solution.py:114
  28.2 1.9 fusion.52
  30.1 27.5 %collective-permute-done = bf16[1024,1024]{1,0:T(8,128)(2,1)} collective-permute-done((bf16[1024,1024]{1,0:T(8,128)(2,1)}, bf16[1024,1024]{1,0:T(8,128)(2,1)}, u32[]{:S(2)}, u32[]{:S(2)}) %collective-permute-start) | collective-permute-done | bytes 2097184 | tf_op jit(solution)/shard_map/ppermute | solution.py:20
  57.7 27.5 %collective-permute-done.1 = bf16[1024,1024]{1,0:T(8,128)(2,1)} collective-permute-done((bf16[1024,1024]{1,0:T(8,128)(2,1)}, bf16[1024,1024]{1,0:T(8,128)(2,1)}, u32[]{:S(2)}, u32[]{:S(2)}) %collective-permute-start.1) | collective-permute-done | bytes 2097184 | tf_op jit(solution)/shard_map/ppermute | solution.py:20
  85.2 27.5 %collective-permute-done.2 = bf16[1024,1024]{1,0:T(8,128)(2,1)S(1)} collective-permute-done((bf16[1024,1024]{1,0:T(8,128)(2,1)}, bf16[1024,1024]{1,0:T(8,128)(2,1)S(1)}, u32[]{:S(2)}, u32[]{:S(2)}) %collective-permute-start.2) | collective-permute-done | bytes 2097184 | tf_op jit(solution)/shard_map/ppermute | solution.py:20
  112.7 1.3 copy-done.1
  114.0 27.3 %collective-permute-done.3 = bf16[1024,1024]{1,0:T(8,128)(2,1)S(1)} collective-permute-done((bf16[1024,1024]{1,0:T(8,128)(2,1)S(1)}, bf16[1024,1024]{1,0:T(8,128)(2,1)S(1)}, u32[]{:S(2)}, u32[]{:S(2)}) %collective-permute-start.3) | collective-permute-done | bytes 2097184 | tf_op jit(solution)/shard_map/ppermute | solution.py:20
  141.3 1.3 copy-done.3
  142.6 27.4 %collective-permute-done.4 = bf16[1024,1024]{1,0:T(8,128)(2,1)} collective-permute-done((bf16[1024,1024]{1,0:T(8,128)(2,1)S(1)}, bf16[1024,1024]{1,0:T(8,128)(2,1)}, u32[]{:S(2)}, u32[]{:S(2)}) %collective-permute-start.4) | collective-permute-done | bytes 2097184 | tf_op jit(solution)/shard_map/ppermute | solution.py:20
  169.9 4.1 fusion.43
  174.1 23.4 %collective-permute-done.5 = bf16[1024,1024]{1,0:T(8,128)(2,1)} collective-permute-done((bf16[1024,1024]{1,0:T(8,128)(2,1)}, bf16[1024,1024]{1,0:T(8,128)(2,1)}, u32[]{:S(2)}, u32[]{:S(2)}) %collective-permute-start.5) | collective-permute-done | bytes 2097184 | tf_op jit(solution)/shard_map/ppermute | solution.py:20
  197.5 3.1 constant_dynamic-update-slice_fusion.1
  200.6 3.2 constant_dynamic-update-slice_fusion
  203.7 6.6 %fusion.46 = f32[384,256]{0,1:T(8,128)S(1)} fusion(bf16[8192,256]{1,0:T(8,128)(2,1)} %constant_dynamic-update-slice_fusion, bf16[384,8192]{1,0:T(8,128)(2,1)} %param.13, f32[8192]{0:T(1024)S(1)} %copy-done.11, f32[384]{0:T(512)S(1)} %add_rsqrt_fusion.1), kind=kOutput, calls=%fused_computation.69 | convolution fusion | flops 1623195648 | bytes 10913280 | tf_op jit(solution)/shard_map/dot_general | solution.py:135
  210.5 14.6 %collective-permute-done.6 = bf16[1024,1024]{1,0:T(8,128)(2,1)} collective-permute-done((bf16[1024,1024]{1,0:T(8,128)(2,1)}, bf16[1024,1024]{1,0:T(8,128)(2,1)}, u32[]{:S(2)}, u32[]{:S(2)}) %collective-permute-start.6) | collective-permute-done | bytes 2097184 | tf_op jit(solution)/shard_map/ppermute | solution.py:20
  225.1 3.1 constant_dynamic-update-slice_fusion.17
  228.1 3.2 constant_dynamic-update-slice_fusion.16
  231.3 3.2 constant_dynamic-update-slice_fusion.15
  234.6 1.5 constant_dynamic-update-slice_fusion.14
  236.0 1.5 constant_dynamic-update-slice_fusion.13
  237.5 3.1 constant_dynamic-update-slice_fusion.12
  240.6 3.1 constant_dynamic-update-slice_fusion.11
  243.7 1.8 constant_dynamic-update-slice_fusion.10
  245.5 3.1 constant_dynamic-update-slice_fusion.9
  248.6 3.0 constant_dynamic-update-slice_fusion.8
  251.6 3.0 constant_dynamic-update-slice_fusion.7
  254.7 1.5 constant_dynamic-update-slice_fusion.6
  256.2 1.5 constant_dynamic-update-slice_fusion.5
  257.7 3.1 constant_dynamic-update-slice_fusion.4
  260.7 3.2 constant_dynamic-update-slice_fusion.3
  263.9 1.9 constant_dynamic-update-slice_fusion.2
  265.8 8.3 %fusion.41 = f32[1024,256]{0,1:T(8,128)S(1)} fusion(bf16[8192,256]{1,0:T(8,128)(2,1)S(1)} %copy-done.7, bf16[1024,16384]{1,0:T(8,128)(2,1)} %constant_dynamic-update-slice_fusion.2, s32[]{:T(128)S(6)} %select_n.221), kind=kOutput, calls=%fused_computation.64 | convolution fusion | flops 4294967296 | bytes 22020100 | tf_op jit(solution)/shard_map/dot_general | solution.py:136
  274.2 0.8 pad_maximum_fusion.1
  275.0 0.3 all-gather.10.cloned.1.call-start
  275.4 0.7 select_reduce_fusion.1
  276.1 0.5 fusion.85
  276.6 0.7 add_convert_fusion.1
  277.3 1.9 multiply_cosine_fusion
  279.2 0.5 fusion.76
  279.7 1.2 fusion.65
  280.8 0.8 maximum_maximum_fusion
  281.7 23.4 %fusion.53 = f32[1024,1024]{0,1:T(8,128)S(1)} fusion(bf16[8192,1024]{1,0:T(8,128)(2,1)} %all-gather.12.cloned.1.call-done, bf16[1024,16384]{1,0:T(8,128)(2,1)} %constant_dynamic-update-slice_fusion.2, s32[]{:T(128)S(6)} %select_n.221, f32[1024]{0:T(1024)S(1)} %copy-done.14), kind=kOutput, calls=%fused_computation.80 | convolution fusion | flops 17180917760 | bytes 37752836 | tf_op jit(solution)/shard_map/dot_general | solution.py:137
  305.1 1.7 fusion.88
  306.8 3.9 copy.30
  310.7 2.7 copy.31
  313.4 4.6 fusion.56
  318.0 2.5 pad_maximum_fusion
  320.5 22.3 %all-gather.10.cloned.1.call-done = bf16[5632,1,128]{0,2,1:T(8,128)(2,1)} async-done(((bf16[1408,1,128]{0,2,1:T(8,128)(2,1)}), bf16[5632,1,128]{0,2,1:T(8,128)(2,1)}) %all-gather.10.cloned.1.call-update) | async-done | bytes 1441808 | tf_op jit(solution)/shard_map/all_gather | solution.py:164
  342.8 207.1 %while.23 = (s32[]{:T(128)}, f32[1024,1,8]{0,2,1:T(8,128)S(1)}, f32[1024,1,8]{0,2,1:T(8,128)}, f32[1024,1,8,128]{0,3,2,1:T(8,128)}, s32[1024]{0:T(1024)}, /*inde...) while((s32[]{:T(128)}, f32[1024,1,8]{0,2,1:T(8,128)S(1)}, ...), condition=%wide.region_8.9_spmd.clone.clone.clone, body=%wide.region_5.8_spmd.clone.clone.clone.sunk | while | flops 12082698240 | bytes 301176576 | solution.py:177
  342.9 5.0 and_select_fusion.2
  348.0 33.8 %fusion.103 = (f32[1024,8]{0,1:T(8,128)S(1)}, f32[2816,1024,8]{1,0,2:T(8,128)}) fusion(pred[1024,2816]{0,1:T(8,128)(4,1)S(1)} %and_select_fusion.2, bf16[1024,1,8,128]{3,0,2,1:T(8,128)(2,1)} %get-tuple-element.550, bf16[5632,1,128]{0,2,1:T(8,128)(2,1)} %get-tuple-element.549, s32[]{:T(128)S(6)} %select_n.313), kind=kOutput, calls=%fused_computation.5.clone.1 | convolution fusion | flops 5974777856 | bytes 98009088 | tf_op jit(solution)/shard_map/while/body/eval_jaxpr/rgqd,ngd->rgqn/dot_general | solution.py:63
  381.8 34.7 %bitcast_add_fusion.5 = f32[1024,1,8,128]{0,3,2,1:T(8,128)} fusion(f32[1024,1,8,128]{0,3,2,1:T(8,128)} %get-tuple-element.534, f32[2816,1024,8]{1,0,2:T(8,128)} %get-tuple-element.516, f32[1024,8]{0,1:T(8,128)S(1)} %bitcast.96, pred[1024,2816]{0,1:T(8,128)(4,1)S(1)} %and_select_fusion.2, f32[1024,8]{0,1:T(8,128)S(1)} %get-tuple-element.517, ...), kind=kOutput, calls=%fused_computation.14.clone.1 | convolution fusion | flops 6001000448 | bytes 104333320 | tf_op jit(solution)/shard_map/while/body/eval_jaxpr/rgqn,ngd->rgqd/dot_general | solution.py:71
  416.5 28.8 %fusion.105 = f32[1024,8]{0,1:T(8,128)S(1)} fusion(f32[2816,1024,8]{1,0,2:T(8,128)} %get-tuple-element.516, f32[1024,8]{0,1:T(8,128)S(1)} %bitcast.97, pred[1024,2816]{0,1:T(8,128)(4,1)S(1)} %and_select_fusion.2), kind=kLoop, calls=%fused_computation.9.clone.1 | loop fusion | flops 92266496 | bytes 95223808 | tf_op jit(solution)/shard_map/while/body/eval_jaxpr/reduce_sum | solution.py:70
  445.4 0.6 copy-done.6
  446.1 5.0 and_select_fusion.2
  451.2 33.8 %fusion.103 = (f32[1024,8]{0,1:T(8,128)S(1)}, f32[2816,1024,8]{1,0,2:T(8,128)}) fusion(pred[1024,2816]{0,1:T(8,128)(4,1)S(1)} %and_select_fusion.2, bf16[1024,1,8,128]{3,0,2,1:T(8,128)(2,1)} %get-tuple-element.550, bf16[5632,1,128]{0,2,1:T(8,128)(2,1)} %get-tuple-element.549, s32[]{:T(128)S(6)} %select_n.313), kind=kOutput, calls=%fused_computation.5.clone.1 | convolution fusion | flops 5974777856 | bytes 98009088 | tf_op jit(solution)/shard_map/while/body/eval_jaxpr/rgqd,ngd->rgqn/dot_general | solution.py:63
  485.0 35.4 %bitcast_add_fusion.5 = f32[1024,1,8,128]{0,3,2,1:T(8,128)} fusion(f32[1024,1,8,128]{0,3,2,1:T(8,128)} %get-tuple-element.534, f32[2816,1024,8]{1,0,2:T(8,128)} %get-tuple-element.516, f32[1024,8]{0,1:T(8,128)S(1)} %bitcast.96, pred[1024,2816]{0,1:T(8,128)(4,1)S(1)} %and_select_fusion.2, f32[1024,8]{0,1:T(8,128)S(1)} %get-tuple-element.517, ...), kind=kOutput, calls=%fused_computation.14.clone.1 | convolution fusion | flops 6001000448 | bytes 104333320 | tf_op jit(solution)/shard_map/while/body/eval_jaxpr/rgqn,ngd->rgqd/dot_general | solution.py:71
  520.4 28.8 %fusion.105 = f32[1024,8]{0,1:T(8,128)S(1)} fusion(f32[2816,1024,8]{1,0,2:T(8,128)} %get-tuple-element.516, f32[1024,8]{0,1:T(8,128)S(1)} %bitcast.97, pred[1024,2816]{0,1:T(8,128)(4,1)S(1)} %and_select_fusion.2), kind=kLoop, calls=%fused_computation.9.clone.1 | loop fusion | flops 92266496 | bytes 95223808 | tf_op jit(solution)/shard_map/while/body/eval_jaxpr/reduce_sum | solution.py:70
  549.3 0.6 copy-done.6
  549.9 2.8 select_convert_fusion
  552.7 2.6 copy.28
  (77 shorter events, 0.9 us)
Async XLA Ops:
  6.5 21.7 %copy-start = (bf16[1024,1024]{1,0:T(8,128)(2,1)S(1)}, bf16[1024,1024]{1,0:T(8,128)(2,1)}, u32[]{:S(2)}) copy-start(bf16[1024,1024]{1,0:T(8,128)(2,1)} %param.14) | copy-start | bytes 6291460
  6.5 191.0 %all-gather.6.cloned.1.call-start = ((), (), s32[]{:S(2)}) async-start(), calls=%async_computation | async-start | bytes 3145728 | tf_op jit(solution)/shard_map/all_gather | solution.py:131
  7.3 193.3 %all-gather.8.cloned.1.call-start = ((), (), s32[]{:S(2)}) async-start(), calls=%async_computation.1 | async-start | bytes 3145728 | tf_op jit(solution)/shard_map/all_gather | solution.py:132
  30.1 27.6 %collective-permute-start = (bf16[1024,1024]{1,0:T(8,128)(2,1)}, bf16[1024,1024]{1,0:T(8,128)(2,1)}, u32[]{:S(2)}, u32[]{:S(2)}) collective-permute-start(bf16[1024,1024]{1,0:T(8,128)(2,1)} %fusion.52), channel_id=1, source_target_pairs={{0,2},{2,4},{4,6},{6,8},{8,10},{10,12},{12,14},{14,0},{1,3},{3,5},... | collective-permute-start | bytes 6291464 | tf_op jit(solution)/shard_map/ppermute | solution.py:20
  30.1 251.6 %all-gather.12.cloned.1.call-start = ((), (), s32[]{:S(2)}) async-start(), calls=%async_computation.3 | async-start | bytes 25165824 | tf_op jit(solution)/shard_map/all_gather | solution.py:133
  57.6 27.6 %collective-permute-start.1 = (bf16[1024,1024]{1,0:T(8,128)(2,1)}, bf16[1024,1024]{1,0:T(8,128)(2,1)}, u32[]{:S(2)}, u32[]{:S(2)}) collective-permute-start(bf16[1024,1024]{1,0:T(8,128)(2,1)} %collective-permute-done), channel_id=1, source_target_pairs={{0,2},{2,4},{4,6},{6,8},{8,10},{10,12},{12,14},{14,0},{1,3},{3,5},... | collective-permute-start | bytes 6291464 | tf_op jit(solution)/shard_map/ppermute | solution.py:20
  57.7 262.8 %all-gather.14.cloned.1.call-start = ((), (), s32[]{:S(2)}) async-start(), calls=%async_computation.4 | async-start | bytes 1802240 | tf_op jit(solution)/shard_map/all_gather | solution.py:165
  85.2 27.5 %collective-permute-start.2 = (bf16[1024,1024]{1,0:T(8,128)(2,1)}, bf16[1024,1024]{1,0:T(8,128)(2,1)S(1)}, u32[]{:S(2)}, u32[]{:S(2)}) collective-permute-start(bf16[1024,1024]{1,0:T(8,128)(2,1)} %collective-permute-done.1), channel_id=1, source_target_pairs={{0,2},{2,4},{4,6},{6,8},{8,10},{10,12},{12,14},{14,0},{1,3},{3,5},... | collective-permute-start | bytes 6291464 | tf_op jit(solution)/shard_map/ppermute | solution.py:20
  112.7 1.3 copy-start.1
  114.0 27.3 %collective-permute-start.3 = (bf16[1024,1024]{1,0:T(8,128)(2,1)S(1)}, bf16[1024,1024]{1,0:T(8,128)(2,1)S(1)}, u32[]{:S(2)}, u32[]{:S(2)}) collective-permute-start(bf16[1024,1024]{1,0:T(8,128)(2,1)S(1)} %collective-permute-done.2), channel_id=1, source_target_pairs={{0,2},{2,4},{4,6},{6,8},{8,10},{10,12},{12,14},{14,0},{1,3},{3,5},... | collective-permute-start | bytes 6291464 | tf_op jit(solution)/shard_map/ppermute | solution.py:20
  141.3 1.3 copy-start.3
  142.6 27.4 %collective-permute-start.4 = (bf16[1024,1024]{1,0:T(8,128)(2,1)S(1)}, bf16[1024,1024]{1,0:T(8,128)(2,1)}, u32[]{:S(2)}, u32[]{:S(2)}) collective-permute-start(bf16[1024,1024]{1,0:T(8,128)(2,1)S(1)} %collective-permute-done.3), channel_id=1, source_target_pairs={{0,2},{2,4},{4,6},{6,8},{8,10},{10,12},{12,14},{14,0},{1,3},{3,5},... | collective-permute-start | bytes 6291464 | tf_op jit(solution)/shard_map/ppermute | solution.py:20
  169.9 27.6 %collective-permute-start.5 = (bf16[1024,1024]{1,0:T(8,128)(2,1)}, bf16[1024,1024]{1,0:T(8,128)(2,1)}, u32[]{:S(2)}, u32[]{:S(2)}) collective-permute-start(bf16[1024,1024]{1,0:T(8,128)(2,1)} %collective-permute-done.4), channel_id=1, source_target_pairs={{0,2},{2,4},{4,6},{6,8},{8,10},{10,12},{12,14},{14,0},{1,3},{3,5},... | collective-permute-start | bytes 6291464 | tf_op jit(solution)/shard_map/ppermute | solution.py:20
  174.1 29.7 %copy-start.11 = (f32[8192]{0:T(1024)S(1)}, f32[8192]{0:T(1024)}, u32[]{:S(2)}) copy-start(f32[8192]{0:T(1024)} %param.15) | copy-start | bytes 98308
  197.5 27.6 %collective-permute-start.6 = (bf16[1024,1024]{1,0:T(8,128)(2,1)}, bf16[1024,1024]{1,0:T(8,128)(2,1)}, u32[]{:S(2)}, u32[]{:S(2)}) collective-permute-start(bf16[1024,1024]{1,0:T(8,128)(2,1)} %collective-permute-done.5), channel_id=1, source_target_pairs={{0,2},{2,4},{4,6},{6,8},{8,10},{10,12},{12,14},{14,0},{1,3},{3,5},... | collective-permute-start | bytes 6291464 | tf_op jit(solution)/shard_map/ppermute | solution.py:20
  203.7 6.6 %copy-start.9 = (f32[128]{0:T(128)S(1)}, f32[128]{0:T(128)}, u32[]{:S(2)}) copy-start(f32[128]{0:T(128)} %param.21) | copy-start | bytes 1540
  203.7 6.6 %copy-start.10 = (f32[128]{0:T(128)S(1)}, f32[128]{0:T(128)}, u32[]{:S(2)}) copy-start(f32[128]{0:T(128)} %param.20) | copy-start | bytes 1540
  228.1 6.4 %copy-start.4 = (bf16[1024,1024]{1,0:T(8,128)(2,1)S(1)}, bf16[1024,1024]{1,0:T(8,128)(2,1)}, u32[]{:S(2)}) copy-start(bf16[1024,1024]{1,0:T(8,128)(2,1)} %copy-done.3) | copy-start | bytes 6291460
  231.3 4.7 copy-start.2
  260.7 5.1 copy-start.7
  265.8 9.6 %copy-start.12 = (s32[16]{0:T(128)S(1)}, s32[16]{0:T(128)}, u32[]{:S(2)}) copy-start(s32[16]{0:T(128)} %param.22) | copy-start | bytes 196
  265.8 9.6 %copy-start.13 = (s32[16]{0:T(128)S(1)}, s32[16]{0:T(128)}, u32[]{:S(2)}) copy-start(s32[16]{0:T(128)} %param.23) | copy-start | bytes 196
  274.1 7.6 %copy-start.14 = (f32[1024]{0:T(1024)S(1)}, f32[1024]{0:T(1024)}, u32[]{:S(2)}) copy-start(f32[1024]{0:T(1024)} %param.19) | copy-start | bytes 12292
  275.0 67.7 %all-gather.10.cloned.1.call-start = ((), (), s32[]{:S(2)}) async-start(), calls=%async_computation.2 | async-start | bytes 1802240 | tf_op jit(solution)/shard_map/all_gather | solution.py:164
  342.8 207.1 %copy-start.8 = (pred[1024]{0:T(1024)(128)(4,1)S(1)}, pred[1024]{0:T(1024)(128)(4,1)}, u32[]{:S(2)}) copy-start(pred[1024]{0:T(1024)(128)(4,1)} %fusion.85) | copy-start | bytes 3076
  416.5 28.9 %copy-start.5 = (f32[1024,1,8]{0,2,1:T(8,128)S(1)}, f32[1024,1,8]{0,2,1:T(8,128)}, u32[]{:S(2)}) copy-start(f32[1024,1,8]{0,2,1:T(8,128)} %get-tuple-element.533) | copy-start | bytes 98308 | tf_op jit(solution)/shard_map/while
  445.4 0.6 copy-start.6
  520.4 28.9 %copy-start.5 = (f32[1024,1,8]{0,2,1:T(8,128)S(1)}, f32[1024,1,8]{0,2,1:T(8,128)}, u32[]{:S(2)}) copy-start(f32[1024,1,8]{0,2,1:T(8,128)} %get-tuple-element.533) | copy-start | bytes 98308 | tf_op jit(solution)/shard_map/while
  549.2 0.6 copy-start.6
Sparse Core Ops, SparseCore 0:
  8.9 35.8 all-gather.5
  46.3 33.0 all-gather.7
  80.9 198.8 all-gather.11
  281.5 29.7 all-gather.13
  313.0 29.7 all-gather.9
